TPU v7x, 512 devices: a whole 4x8x8 slice. The times are simulated.
512 devices in a mesh: grp: 16 (over y, core), path: 32 (over z, x).
Axes of the slice: x: 4, y: 8, z: 8, core: 2. Of those that a mesh axis runs over, the one named last changes fastest.
Arguments:
- link_state: bfloat16 [16, 16384, 256], P('grp', 'path'), may hold values from -6 to 6
- path_state: bfloat16 [16, 4096, 256], P('grp', 'path'), may hold values from -6 to 6
- path_links: int32 [4096, 8], P('path'), may hold values from -1 to 16383, as said below
- w_path_in: bfloat16 [256, 768], replicated, may hold values from -0.375 to 0.375
- w_path_hid: bfloat16 [256, 768], replicated, may hold values from -0.375 to 0.375
- w_link_in: bfloat16 [256, 768], replicated, may hold values from -0.375 to 0.375
- w_link_hid: bfloat16 [256, 768], replicated, may hold values from -0.375 to 0.375
- cotangent: bfloat16 [16, 4096, 128], P('grp', 'path'), may hold values from -0.0234375 to 0.0234375
Outputs:
- link_next: bfloat16 [16, 16384, 256], P('grp', 'path')
- path_final: bfloat16 [16, 4096, 256], P('grp', 'path')
- read_grad: float32 [128, 256], P('path')
Inputs may be any that keep to these rules, and one draw needn't show every extreme that they name: `path_links`: entry -1 marks no hop; each path's live entries come first and number two or more. In the rows of one device, at most 32 live entries name links of the block of 512 link ids held by any one index of path, and some block takes exactly 32.
All inputs are finite; a program needn't handle non-finite values.
Results may differ from a plain program's by a relative error of at most 0.0035.
Values may be sent and summed in bfloat16 or wider, within the bound.
A program may use at most 64 MiB of HBM per device.

v0:
```python
import jax
import jax.numpy as jnp
from jax import lax
from jax.sharding import PartitionSpec as P


def gated_update(projected, carried, w_hidden):
    width = carried.shape[1]
    recur = jnp.dot(carried.astype(jnp.bfloat16), w_hidden, preferred_element_type=jnp.float32)
    reset = jax.nn.sigmoid(projected[:, :width] + recur[:, :width])
    update = jax.nn.sigmoid(projected[:, width : 2 * width] + recur[:, width : 2 * width])
    candidate = jnp.tanh(projected[:, 2 * width :] + reset * recur[:, 2 * width :])
    return (1.0 - update) * candidate + update * carried


def shards(
    link_state, path_state, path_links, w_path_in, w_path_hid, w_link_in, w_link_hid, cotangent
):
    bf16, f32 = (jnp.bfloat16, jnp.float32)
    own_links = link_state[0]
    link_dev, width = own_links.shape
    peer_count = lax.axis_size("path")
    path_count, hop_count = path_links.shape
    entries = path_count * hop_count
    capacity = entries // peer_count
    slots = peer_count * capacity
    flat_ids = path_links.reshape(-1)
    is_live = flat_ids >= 0
    owner_id = jnp.where(is_live, flat_ids // link_dev, peer_count)
    local_id = jnp.where(is_live, flat_ids % link_dev, 0)
    marks = (owner_id[:, None] == jnp.arange(peer_count)[None, :]).astype(bf16)
    order = jnp.arange(entries)
    earlier = (order[None, :] < order[:, None]).astype(bf16)
    before = jnp.dot(earlier, marks, preferred_element_type=f32)
    slot_id = jnp.sum(before * marks.astype(f32), axis=1).astype(jnp.int32)
    dest = jnp.where(is_live, owner_id * capacity + slot_id, -1)
    slot_ids = jnp.arange(slots)
    route = dest[None, :] == slot_ids[:, None]
    requests = jnp.sum(jnp.where(route, local_id[None, :] + 1, 0), axis=1) - 1
    received = lax.all_to_all(
        requests.reshape(peer_count, capacity), "path", split_axis=0, concat_axis=0, tiled=True
    ).reshape(-1)
    want = (received[:, None] == jnp.arange(link_dev)[None, :]).astype(bf16)
    served = jnp.dot(want, own_links, preferred_element_type=f32).astype(bf16)
    got = lax.all_to_all(
        served.reshape(peer_count, capacity, width), "path", split_axis=0, concat_axis=0, tiled=True
    ).reshape(slots, width)
    route_t = (dest[:, None] == slot_ids[None, :]).astype(bf16)
    fetched = jnp.dot(route_t, got, preferred_element_type=f32).astype(bf16)
    projected = jnp.dot(fetched, w_path_in, preferred_element_type=f32)
    projected = projected.reshape(path_count, hop_count, 3 * width)
    live_grid = is_live.reshape(path_count, hop_count)
    carried = path_state[0].astype(f32)
    messages = []
    for hop_index in range(hop_count):
        renewed = gated_update(projected[:, hop_index], carried, w_path_hid)
        carried = jnp.where(live_grid[:, hop_index, None], renewed, carried)
        messages.append(carried.astype(bf16))
    path_final = carried.astype(bf16)
    flat_messages = jnp.stack(messages, axis=1).reshape(-1, width)
    outgoing = jnp.dot(route.astype(bf16), flat_messages, preferred_element_type=f32).astype(bf16)
    incoming = lax.all_to_all(
        outgoing.reshape(peer_count, capacity, width),
        "path",
        split_axis=0,
        concat_axis=0,
        tiled=True,
    ).reshape(slots, width)
    link_sum = lax.dot_general(want, incoming, (((0,), (0,)), ((), ())), preferred_element_type=f32)
    link_proj = jnp.dot(link_sum.astype(bf16), w_link_in, preferred_element_type=f32)
    link_next = gated_update(link_proj, own_links.astype(f32), w_link_hid).astype(bf16)
    grad_term = lax.dot_general(
        cotangent[0], path_final, (((0,), (0,)), ((), ())), preferred_element_type=f32
    )
    part = lax.psum_scatter(grad_term, "path", scatter_dimension=0, tiled=True)
    read_grad = lax.psum(part, "grp")
    return (link_next[None], path_final[None], read_grad)


def solution(mesh):
    return jax.shard_map(
        shards,
        mesh=mesh,
        in_specs=(
            P("grp", "path", None),
            P("grp", "path", None),
            P("path", None),
            P(),
            P(),
            P(),
            P(),
            P("grp", "path", None),
        ),
        out_specs=(P("grp", "path", None), P("grp", "path", None), P("path", None)),
        check_vma=False,
    )
```

profile of v0, /device:TPU:2, one launch (start us, length us, event | category | flops | bytes accessed | tf_op | source)
XLA Modules:
  0.0 300.5 jit_solution(5889730820409296890)
XLA Ops:
  7.2 0.9 copy.42
  8.2 0.5 fusion.13
  8.7 0.5 select_reduce_fusion
  9.3 21.8 %all_to_all.16 = s32[32,1,32]{2,1,0:T(1,128)S(1)} all-to-all(s32[32,1,32]{2,1,0:T(1,128)S(1)} %sub.41), channel_id=1, replica_groups=mesh['grp'=16,'path'=32] {'path'}, dimensions={0} | all-to-all | bytes 8192 | tf_op jit(solution)/shard_map/all_to_all | solution.py:40
  31.1 0.5 broadcast.189
  31.6 0.7 reduce.3
  32.4 2.3 fusion.7
  34.7 5.0 %all-to-all-start.1 = ((bf16[32,32,256]{2,1,0:T(8,128)(2,1)}), bf16[32,32,256]{2,1,0:T(8,128)(2,1)S(1)}, u32[]{:S(2)}, u32[]{:S(2)}) async-start(bf16[32,32,256]{2,1,0:T(8,128)(2,1)} %bitcast.2), calls=%async_computation.1 | async-start | bytes 1048576 | tf_op jit(solution)/shard_map/all_to_all | solution.py:45
  39.7 0.2 fusion.141
  39.9 15.5 %all-to-all-done.1 = bf16[32,32,256]{2,1,0:T(8,128)(2,1)S(1)} async-done(((bf16[32,32,256]{2,1,0:T(8,128)(2,1)}), bf16[32,32,256]{2,1,0:T(8,128)(2,1)S(1)}, u32[]{:S(2)}, u32[]{:S(2)}) %all-to-all-start.1) | async-done | bytes 524320 | tf_op jit(solution)/shard_map/all_to_all | solution.py:45
  55.4 3.5 %convolution_bitcast_fusion = f32[128,8,768]{2,1,0:T(8,128)} fusion(bf16[256,768]{1,0:T(8,128)(2,1)S(1)} %copy-done, bf16[1024,256]{1,0:T(8,128)(2,1)S(1)} %bitcast.96, s32[1024]{0:T(1024)S(1)} %add_select_fusion.2), kind=kOutput, calls=%fused_computation.12 | convolution fusion | flops 940834816 | bytes 4067328 | tf_op jit(solution)/shard_map/dot_general | solution.py:50
  58.9 13.3 %fusion.171 = (f32[128,1,768]{2,1,0:T(1,128)S(1)}, f32[128,1,768]{2,1,0:T(1,128)S(1)}, f32[128,1,768]{2,1,0:T(1,128)S(1)}, f32[128,1,768]{2,1,0:T(1,128)S(1)}, f...) fusion(f32[128,8,768]{2,1,0:T(8,128)} %convolution_bitcast_fusion), kind=kLoop, calls=%fused_computation.235 | loop fusion | bytes 6291456 | tf_op jit(solution)/shard_map/slice | solution.py:56
  72.4 0.2 fusion.157
  72.7 0.2 fusion.155
  73.1 0.2 fusion.153
  73.5 0.2 fusion.151
  73.9 0.2 fusion.149
  74.2 0.2 fusion.147
  74.6 0.2 fusion.145
  74.9 0.1 bitcast_dynamic-update-slice_fusion
  75.0 1.8 fusion.9
  76.8 5.6 %all-to-all-start.2 = ((bf16[32,32,256]{2,1,0:T(8,128)(2,1)}), bf16[32,32,256]{2,1,0:T(8,128)(2,1)S(1)}, u32[]{:S(2)}, u32[]{:S(2)}) async-start(bf16[32,32,256]{2,1,0:T(8,128)(2,1)} %bitcast.30), calls=%async_computation.2 | async-start | bytes 1048576 | tf_op jit(solution)/shard_map/all_to_all | solution.py:62
  82.4 0.9 convolution_bitcast_fusion.1
  83.3 0.4 fusion.32
  83.7 1.3 dynamic-slice
  85.6 154.7 %all-reduce.3.cloned.1.call-done = f32[128,256]{0,1:T(8,128)} async-done(((f32[128,256]{0,1:T(8,128)}), f32[128,256]{0,1:T(8,128)}) %all-reduce.3.cloned.1.call-update) | async-done | bytes 131088
  240.3 1.0 constant_dynamic-slice_fusion
  241.3 46.5 %psum.7 = f32[4,256]{0,1:T(8,128)S(1)} all-reduce(f32[4,256]{0,1:T(8,128)S(1)} %constant_dynamic-slice_fusion), channel_id=1, replica_groups=mesh['grp'=16,'path'=32] {'grp'}, use_global_device_ids=true, to_apply=%region_3.4 | all-reduce | flops 1024 | bytes 8192 | tf_op jit(solution)/shard_map/psum | solution.py:76
  287.8 0.7 copy.52
  288.5 0.8 copy-done.2
  289.3 2.4 fusion.11
  291.7 2.0 fusion.35
  (39 shorter events, 1.4 us)
Async XLA Ops:
  7.2 48.3 %copy-start = (bf16[256,768]{1,0:T(8,128)(2,1)S(1)}, bf16[256,768]{1,0:T(8,128)(2,1)}, u32[]{:S(2)}) copy-start(bf16[256,768]{1,0:T(8,128)(2,1)} %param.11) | copy-start | bytes 1179652
  7.2 32.5 %copy-start.8 = (s32[128,8]{0,1:T(8,128)S(1)}, s32[128,8]{0,1:T(8,128)}, u32[]{:S(2)}) copy-start(s32[128,8]{0,1:T(8,128)} %param.10) | copy-start | bytes 12292
  7.2 32.5 %copy-start.1 = (bf16[256,768]{1,0:T(8,128)(2,1)S(1)}, bf16[256,768]{1,0:T(8,128)(2,1)}, u32[]{:S(2)}) copy-start(bf16[256,768]{1,0:T(8,128)(2,1)} %param.12) | copy-start | bytes 1179652
  7.2 32.5 %copy-start.6 = (bf16[1,128,256]{2,1,0:T(8,128)(2,1)S(1)}, bf16[1,128,256]{2,1,0:T(8,128)(2,1)}, u32[]{:S(2)}) copy-start(bf16[1,128,256]{2,1,0:T(8,128)(2,1)} %param.9) | copy-start | bytes 196612
  34.7 20.8 %all-to-all-start.1 = ((bf16[32,32,256]{2,1,0:T(8,128)(2,1)}), bf16[32,32,256]{2,1,0:T(8,128)(2,1)S(1)}, u32[]{:S(2)}, u32[]{:S(2)}) async-start(bf16[32,32,256]{2,1,0:T(8,128)(2,1)} %bitcast.2), calls=%async_computation.1 | async-start | bytes 1048576 | tf_op jit(solution)/shard_map/all_to_all | solution.py:45
  74.6 7.8 %copy-start.7 = (bf16[1,128,128]{2,1,0:T(8,128)(2,1)S(1)}, bf16[1,128,128]{2,1,0:T(8,128)(2,1)}, u32[]{:S(2)}) copy-start(bf16[1,128,128]{2,1,0:T(8,128)(2,1)} %param.15) | copy-start | bytes 98308
  74.9 8.5 %copy-start.3 = (bf16[1,512,256]{2,1,0:T(8,128)(2,1)S(1)}, bf16[1,512,256]{2,1,0:T(8,128)(2,1)}, u32[]{:S(2)}) copy-start(bf16[1,512,256]{2,1,0:T(8,128)(2,1)} %param.8) | copy-start | bytes 786436
  74.9 8.5 %copy-start.4 = (bf16[256,768]{1,0:T(8,128)(2,1)S(1)}, bf16[256,768]{1,0:T(8,128)(2,1)}, u32[]{:S(2)}) copy-start(bf16[256,768]{1,0:T(8,128)(2,1)} %param.14) | copy-start | bytes 1179652
  75.0 8.3 %copy-start.5 = (bf16[128,256]{1,0:T(8,128)(2,1)}, bf16[128,256]{1,0:T(8,128)(2,1)S(1)}, u32[]{:S(2)}) copy-start(bf16[128,256]{1,0:T(8,128)(2,1)S(1)} %get-tuple-element.16) | copy-start | bytes 196612
  76.8 211.7 %all-to-all-start.2 = ((bf16[32,32,256]{2,1,0:T(8,128)(2,1)}), bf16[32,32,256]{2,1,0:T(8,128)(2,1)S(1)}, u32[]{:S(2)}, u32[]{:S(2)}) async-start(bf16[32,32,256]{2,1,0:T(8,128)(2,1)} %bitcast.30), calls=%async_computation.2 | async-start | bytes 1048576 | tf_op jit(solution)/shard_map/all_to_all | solution.py:62
  82.4 157.9 %all-reduce.3.cloned.1.call-start = ((), (), s32[]{:S(2)}) async-start(), calls=%async_computation.3 | async-start | bytes 262144
  288.5 0.8 copy-start.2
Sparse Core Ops, SparseCore 0:
  87.2 153.0 all-reduce.2
where the time goes:
time: 301 us
  waiting for transfers between devices  170 us (56%)
  blocking collectives  68.2 us (23%)
  local copies, waits for them, and re-layouts  18.9 us (6%)
  between operations  15 us (5%)
  matrix products  13.4 us (4%)
  starting transfers between devices  10.6 us (4%)
  other arithmetic  4.16 us (1%)
    unnamed x2, waiting for transfers between devices  155 us
    psum x1, blocking collectives, shards(): read_grad = lax.psum(part, 'grp')  46.5 us
    all_to_all x1, blocking collectives, shards(): lax.all_to_all(requests.reshape(peer_count, capacity), 'path', split_axis...  21.8 us
    all_to_all x1, waiting for transfers between devices, shards(): lax.all_to_all(served.reshape(peer_count, capacity, width), 'path', split...  15.5 us
    slice x1, local copies, waits for them, and re-layouts, shards(): renewed = gated_update(projected[:, hop_index], carried, w_path_hid)  13.3 us
  transfers between devices with their start and end apart: 3, of which 2 were waited for; matrix products, arithmetic and copies ran while one was open for 1% of the time, Pallas kernels for 0%

commit v1 on v0

--- a/solution.py
+++ b/solution.py
@@ -73,7 +73,7 @@
         cotangent[0], path_final, (((0,), (0,)), ((), ())), preferred_element_type=f32
     )
     part = lax.psum_scatter(grad_term, "path", scatter_dimension=0, tiled=True)
-    read_grad = lax.psum(part, "grp")
+    read_grad = jnp.sum(lax.all_gather(part, "grp"), axis=0)
     return (link_next[None], path_final[None], read_grad)
 
 

time: 301 us -> 273 us (0.907)
  the two profiles are of different devices: /device:TPU:2 before, /device:TPU:1 now
where the time goes in v1:
time: 273 us
  waiting for transfers between devices  167 us (61%)
  blocking collectives  43.8 us (16%)
  local copies, waits for them, and re-layouts  18.3 us (7%)
  between operations  15 us (5%)
  matrix products  13.4 us (5%)
  starting transfers between devices  10.2 us (4%)
  other arithmetic  4.78 us (2%)
    unnamed x2, waiting for transfers between devices  153 us
    all_to_all x1, blocking collectives, shards(): lax.all_to_all(requests.reshape(peer_count, capacity), 'path', split_axis...  22.1 us
    all_gather x1, blocking collectives, shards(): read_grad = jnp.sum(lax.all_gather(part, 'grp'), axis=0)  21.7 us
    all_to_all x1, waiting for transfers between devices, shards(): lax.all_to_all(served.reshape(peer_count, capacity, width), 'path', split...  14.4 us
    slice x1, local copies, waits for them, and re-layouts, shards(): renewed = gated_update(projected[:, hop_index], carried, w_path_hid)  13.3 us
    all_to_all x1, starting transfers between devices, shards(): lax.all_to_all(outgoing.reshape(peer_count, capacity, width), 'path', spl...  6.3 us
  transfers between devices with their start and end apart: 3, of which 2 were waited for; matrix products, arithmetic and copies ran while one was open for 2% of the time, Pallas kernels for 0%

profile of v1, /device:TPU:1, one launch (start us, length us, event | category | flops | bytes accessed | tf_op | source)
XLA Modules:
  0.0 272.6 jit_solution(6424181043531358821)
XLA Ops:
  7.2 0.9 copy.42
  8.2 0.5 fusion.13
  8.7 0.5 select_reduce_fusion
  9.3 22.1 %all_to_all.16 = s32[32,1,32]{2,1,0:T(1,128)S(1)} all-to-all(s32[32,1,32]{2,1,0:T(1,128)S(1)} %sub.41), channel_id=1, replica_groups=mesh['grp'=16,'path'=32] {'path'}, dimensions={0} | all-to-all | bytes 8192 | tf_op jit(solution)/shard_map/all_to_all | solution.py:40
  31.4 0.5 broadcast.189
  31.9 0.7 reduce.4
  32.7 2.3 fusion.7
  35.0 3.9 %all-to-all-start.1 = ((bf16[32,32,256]{2,1,0:T(8,128)(2,1)}), bf16[32,32,256]{2,1,0:T(8,128)(2,1)S(1)}, u32[]{:S(2)}, u32[]{:S(2)}) async-start(bf16[32,32,256]{2,1,0:T(8,128)(2,1)} %bitcast.2), calls=%async_computation.1 | async-start | bytes 1048576 | tf_op jit(solution)/shard_map/all_to_all | solution.py:45
  38.9 0.2 fusion.141
  39.2 14.4 %all-to-all-done.1 = bf16[32,32,256]{2,1,0:T(8,128)(2,1)S(1)} async-done(((bf16[32,32,256]{2,1,0:T(8,128)(2,1)}), bf16[32,32,256]{2,1,0:T(8,128)(2,1)S(1)}, u32[]{:S(2)}, u32[]{:S(2)}) %all-to-all-start.1) | async-done | bytes 524320 | tf_op jit(solution)/shard_map/all_to_all | solution.py:45
  53.5 3.5 %convolution_bitcast_fusion = f32[128,8,768]{2,1,0:T(8,128)} fusion(bf16[256,768]{1,0:T(8,128)(2,1)S(1)} %copy-done, bf16[1024,256]{1,0:T(8,128)(2,1)S(1)} %bitcast.98, s32[1024]{0:T(1024)S(1)} %add_select_fusion.2), kind=kOutput, calls=%fused_computation.12 | convolution fusion | flops 940834816 | bytes 4067328 | tf_op jit(solution)/shard_map/dot_general | solution.py:50
  57.0 13.3 %fusion.171 = (f32[128,1,768]{2,1,0:T(1,128)S(1)}, f32[128,1,768]{2,1,0:T(1,128)S(1)}, f32[128,1,768]{2,1,0:T(1,128)S(1)}, f32[128,1,768]{2,1,0:T(1,128)S(1)}, f...) fusion(f32[128,8,768]{2,1,0:T(8,128)} %convolution_bitcast_fusion), kind=kLoop, calls=%fused_computation.235 | loop fusion | bytes 6291456 | tf_op jit(solution)/shard_map/slice | solution.py:56
  70.5 0.2 fusion.157
  70.8 0.2 fusion.155
  71.2 0.2 fusion.153
  71.6 0.2 fusion.151
  72.0 0.2 fusion.149
  72.3 0.2 fusion.147
  72.7 0.2 fusion.145
  73.0 0.1 bitcast_dynamic-update-slice_fusion
  73.1 1.8 fusion.9
  74.9 6.3 %all-to-all-start.2 = ((bf16[32,32,256]{2,1,0:T(8,128)(2,1)}), bf16[32,32,256]{2,1,0:T(8,128)(2,1)S(1)}, u32[]{:S(2)}, u32[]{:S(2)}) async-start(bf16[32,32,256]{2,1,0:T(8,128)(2,1)} %bitcast.30), calls=%async_computation.2 | async-start | bytes 1048576 | tf_op jit(solution)/shard_map/all_to_all | solution.py:62
  81.3 0.9 convolution_bitcast_fusion.1
  82.2 0.4 fusion.32
  82.5 1.3 dynamic-slice
  84.5 152.6 %all-reduce.3.cloned.1.call-done = f32[128,256]{0,1:T(8,128)} async-done(((f32[128,256]{0,1:T(8,128)}), f32[128,256]{0,1:T(8,128)}) %all-reduce.3.cloned.1.call-update) | async-done | bytes 131088
  237.1 1.0 dynamic-slice_bitcast_fusion
  238.2 21.7 %all-gather.1 = f32[16,4,256]{2,1,0:T(4,128)S(1)} all-gather(f32[1,4,256]{2,1,0:T(4,128)S(1)} %copy.52), channel_id=2, replica_groups=mesh['grp'=16,'path'=32] {'grp'}, dimensions={0}, use_global_device_ids=true | all-gather | bytes 69632 | tf_op jit(solution)/shard_map/all_gather | solution.py:76
  259.9 0.6 reduce_sum.29
  260.5 0.8 copy-done.2
  261.3 2.4 fusion.11
  263.7 2.0 fusion.35
  (40 shorter events, 1.5 us)
Async XLA Ops:
  7.2 46.4 %copy-start = (bf16[256,768]{1,0:T(8,128)(2,1)S(1)}, bf16[256,768]{1,0:T(8,128)(2,1)}, u32[]{:S(2)}) copy-start(bf16[256,768]{1,0:T(8,128)(2,1)} %param.11) | copy-start | bytes 1179652
  7.2 31.7 %copy-start.8 = (s32[128,8]{0,1:T(8,128)S(1)}, s32[128,8]{0,1:T(8,128)}, u32[]{:S(2)}) copy-start(s32[128,8]{0,1:T(8,128)} %param.10) | copy-start | bytes 12292
  7.2 31.7 %copy-start.1 = (bf16[256,768]{1,0:T(8,128)(2,1)S(1)}, bf16[256,768]{1,0:T(8,128)(2,1)}, u32[]{:S(2)}) copy-start(bf16[256,768]{1,0:T(8,128)(2,1)} %param.12) | copy-start | bytes 1179652
  7.2 31.7 %copy-start.6 = (bf16[1,128,256]{2,1,0:T(8,128)(2,1)S(1)}, bf16[1,128,256]{2,1,0:T(8,128)(2,1)}, u32[]{:S(2)}) copy-start(bf16[1,128,256]{2,1,0:T(8,128)(2,1)} %param.9) | copy-start | bytes 196612
  35.0 18.5 %all-to-all-start.1 = ((bf16[32,32,256]{2,1,0:T(8,128)(2,1)}), bf16[32,32,256]{2,1,0:T(8,128)(2,1)S(1)}, u32[]{:S(2)}, u32[]{:S(2)}) async-start(bf16[32,32,256]{2,1,0:T(8,128)(2,1)} %bitcast.2), calls=%async_computation.1 | async-start | bytes 1048576 | tf_op jit(solution)/shard_map/all_to_all | solution.py:45
  72.7 8.5 %copy-start.7 = (bf16[1,128,128]{2,1,0:T(8,128)(2,1)S(1)}, bf16[1,128,128]{2,1,0:T(8,128)(2,1)}, u32[]{:S(2)}) copy-start(bf16[1,128,128]{2,1,0:T(8,128)(2,1)} %param.15) | copy-start | bytes 98308
  73.0 9.2 %copy-start.3 = (bf16[1,512,256]{2,1,0:T(8,128)(2,1)S(1)}, bf16[1,512,256]{2,1,0:T(8,128)(2,1)}, u32[]{:S(2)}) copy-start(bf16[1,512,256]{2,1,0:T(8,128)(2,1)} %param.8) | copy-start | bytes 786436
  73.0 9.2 %copy-start.4 = (bf16[256,768]{1,0:T(8,128)(2,1)S(1)}, bf16[256,768]{1,0:T(8,128)(2,1)}, u32[]{:S(2)}) copy-start(bf16[256,768]{1,0:T(8,128)(2,1)} %param.14) | copy-start | bytes 1179652
  73.1 9.0 %copy-start.5 = (bf16[128,256]{1,0:T(8,128)(2,1)}, bf16[128,256]{1,0:T(8,128)(2,1)S(1)}, u32[]{:S(2)}) copy-start(bf16[128,256]{1,0:T(8,128)(2,1)S(1)} %get-tuple-element.10) | copy-start | bytes 196612
  74.9 185.6 %all-to-all-start.2 = ((bf16[32,32,256]{2,1,0:T(8,128)(2,1)}), bf16[32,32,256]{2,1,0:T(8,128)(2,1)S(1)}, u32[]{:S(2)}, u32[]{:S(2)}) async-start(bf16[32,32,256]{2,1,0:T(8,128)(2,1)} %bitcast.30), calls=%async_computation.2 | async-start | bytes 1048576 | tf_op jit(solution)/shard_map/all_to_all | solution.py:62
  81.2 155.9 %all-reduce.3.cloned.1.call-start = ((), (), s32[]{:S(2)}) async-start(), calls=%async_computation.3 | async-start | bytes 262144
  260.5 0.8 copy-start.2
Sparse Core Ops, SparseCore 0:
  86.1 150.9 all-reduce.2
